TPU v7x, 32 devices: a whole 2x2x4 slice. The times are simulated.
32 devices in a mesh: fsdp: 16 (over z, x, core), dp: 2 (over y).
Axes of the slice: x: 2, y: 2, z: 4, core: 2. Of those that a mesh axis runs over, the one named last changes fastest.
Arguments:
- tokens: bfloat16 [32768, 768], P(('fsdp', 'dp')), may hold values from -6 to 6
- segment_ids: int32 [32, 1024], P(('fsdp', 'dp')), may hold values from -1 to 15, as said below
- projection: float32 [12, 32, 64], replicated, may hold values from -0.75 to 0.75
- norm1_gain: bfloat16 [768], P('fsdp'), may hold values from 0.5 to 1.5
- norm1_bias: bfloat16 [768], P('fsdp'), may hold values from -1.1953125 to 1.1953125
- qkv_weight: bfloat16 [768, 2304], P('fsdp'), may hold values from -0.21875 to 0.21875
- qkv_bias: bfloat16 [2304], P('fsdp'), may hold values from -1.1953125 to 1.1953125
- out_weight: bfloat16 [768, 768], P('fsdp'), may hold values from -1.5 to 1.5
- out_bias: bfloat16 [768], P('fsdp'), may hold values from -1.1953125 to 1.1953125
- norm2_gain: bfloat16 [768], P('fsdp'), may hold values from 0.5 to 1.5
- norm2_bias: bfloat16 [768], P('fsdp'), may hold values from -1.1953125 to 1.1953125
- in_weight: bfloat16 [768, 3072], P('fsdp'), may hold values from -0.21875 to 0.21875
- in_bias: bfloat16 [3072], P('fsdp'), may hold values from -1.1953125 to 1.1953125
- ffn_out_weight: bfloat16 [3072, 768], P('fsdp'), may hold values from -0.109375 to 0.109375
- ffn_out_bias: bfloat16 [768], P('fsdp'), may hold values from -1.1953125 to 1.1953125
- cotangent: bfloat16 [32768, 768], P(('fsdp', 'dp')), may hold values from -6 to 6
Outputs:
- output: bfloat16 [32768, 768], P(('fsdp', 'dp'))
- tokens_grad: bfloat16 [32768, 768], P(('fsdp', 'dp'))
- norm1_gain_grad: float32 [768], P('fsdp')
- norm1_bias_grad: float32 [768], P('fsdp')
- qkv_weight_grad: float32 [768, 2304], P('fsdp')
- query_key_bias_grad: float32 [1536], P('fsdp')
- value_bias_grad: float32 [768], P('fsdp')
- out_weight_grad: float32 [768, 768], P('fsdp')
- out_bias_grad: float32 [768], P('fsdp')
- norm2_gain_grad: float32 [768], P('fsdp')
- norm2_bias_grad: float32 [768], P('fsdp')
- in_weight_grad: float32 [768, 3072], P('fsdp')
- in_bias_grad: float32 [3072], P('fsdp')
- ffn_out_weight_grad: float32 [3072, 768], P('fsdp')
- ffn_out_bias_grad: float32 [768], P('fsdp')
Inputs may be any that keep to these rules, and one draw needn't show every extreme that they name: `segment_ids`: in each sequence the ids never fall until the padding; the last 1 to 256 rows of every sequence are -1 and no others; every sequence reaches id 16 - 1; some segments may have no rows.
All inputs are finite; a program needn't handle non-finite values.
Results may differ from a plain program's by a relative error of at most 0.01.
Values may be sent and summed in bfloat16 or wider, within the bound.
A program may use at most 192 MiB of HBM per device.

v0:
```python
import jax
import jax.numpy as jnp
from jax import lax
from jax.sharding import PartitionSpec as P

HEADS = 12
HEAD_DIM = 64
SEGS = 16
highest = lax.Precision.HIGHEST
epsilon = 1e-05


def norm_forward(rows, gain, shift):
    row_mean = jnp.mean(rows, axis=-1, keepdims=True)
    centred = rows - row_mean
    inv_std = lax.rsqrt(jnp.mean(centred * centred, axis=-1, keepdims=True) + epsilon)
    normed = centred * inv_std
    return (normed * gain + shift, normed, inv_std)


def norm_backward(incoming, normed, inv_std, gain):
    scaled = incoming * gain
    mean_one = jnp.mean(scaled, axis=-1, keepdims=True)
    mean_two = jnp.mean(scaled * normed, axis=-1, keepdims=True)
    input_grad = inv_std * (scaled - mean_one - normed * mean_two)
    return (input_grad, jnp.sum(incoming * normed, axis=0), jnp.sum(incoming, axis=0))


def rotary_tables(length, half_width):
    positions = jnp.arange(length, dtype=jnp.float32)
    frequency = 10000.0 ** (-jnp.arange(half_width, dtype=jnp.float32) / half_width)
    angles = positions[:, None] * frequency[None, :]
    return (jnp.cos(angles)[:, None, :], jnp.sin(angles)[:, None, :])


def rotate(values, cosine, sine):
    half_width = values.shape[-1] // 2
    lower_half = values[..., :half_width]
    upper_half = values[..., half_width:]
    return jnp.concatenate(
        [lower_half * cosine - upper_half * sine, lower_half * sine + upper_half * cosine], axis=-1
    )


def segment_core(query_rows, key_rows, value_rows, segment, projection):
    length = query_rows.shape[0]
    cosine, sine = rotary_tables(length, query_rows.shape[-1] // 2)
    feat_query = jax.nn.softplus(
        jnp.einsum("nhd,hfd->nhf", rotate(query_rows, cosine, sine), projection, precision=highest)
    )
    feat_key = jax.nn.softplus(
        jnp.einsum("nhd,hfd->nhf", rotate(key_rows, cosine, sine), projection, precision=highest)
    )
    member = (segment[:, None] == jnp.arange(SEGS, dtype=jnp.int32)[None, :]).astype(jnp.float32)
    present = jnp.sum(member, axis=-1)
    masked_keys = member[:, :, None, None] * feat_key[:, None]
    kv_state = jnp.einsum("nshf,nhd->shfd", masked_keys, value_rows, precision=highest)
    totals = jnp.sum(masked_keys, axis=0)
    masked_queries = member[:, :, None, None] * feat_query[:, None]
    numerator = jnp.einsum("nshf,shfd->nhd", masked_queries, kv_state, precision=highest)
    denominator = (
        jnp.einsum("nshf,shf->nh", masked_queries, totals, precision=highest)
        + (1.0 - present)[:, None]
    )
    return numerator / denominator[:, :, None]


def attend(projected, segment_ids, projection):
    seq_count, length = segment_ids.shape
    shaped = projected.reshape(seq_count, length, 3, HEADS, HEAD_DIM)

    def one_sequence(pieces):
        rows, segment = pieces
        return segment_core(rows[:, 0], rows[:, 1], rows[:, 2], segment, projection)

    return lax.map(one_sequence, (shaped, segment_ids)).reshape(
        seq_count * length, HEADS * HEAD_DIM
    )


def attend_back(projected, segment_ids, projection, grad_attended):
    seq_count, length = segment_ids.shape
    shaped = projected.reshape(seq_count, length, 3, HEADS, HEAD_DIM)
    upstream_rows = grad_attended.reshape(seq_count, length, HEADS, HEAD_DIM)

    def one_sequence(pieces):
        rows, segment, upstream = pieces

        def local_core(query_rows, key_rows, value_rows):
            return segment_core(query_rows, key_rows, value_rows, segment, projection)

        unused, pull = jax.vjp(local_core, rows[:, 0], rows[:, 1], rows[:, 2])
        grads = pull(upstream)
        return jnp.stack(grads, axis=1)

    result = lax.map(one_sequence, (shaped, segment_ids, upstream_rows))
    return result.reshape(seq_count * length, 3 * HEADS * HEAD_DIM)


def contract_rows(left, right):
    return lax.dot_general(
        left, right, (((0,), (0,)), ((), ())), preferred_element_type=jnp.float32
    )


def contract_cols(left, right):
    return lax.dot_general(
        left, right, (((1,), (1,)), ((), ())), preferred_element_type=jnp.float32
    )


def fetch_block(params):
    return (
        lax.all_gather(params[0], "fsdp", axis=0, tiled=True),
        lax.all_gather(params[1], "fsdp", axis=0, tiled=True),
        lax.all_gather(params[2], "fsdp", axis=0, tiled=True),
        lax.all_gather(params[3], "fsdp", axis=0, tiled=True),
        lax.all_gather(params[4], "fsdp", axis=0, tiled=True),
        lax.all_gather(params[5], "fsdp", axis=0, tiled=True),
    )


def backward_weights(params):
    return (
        lax.all_gather(params[0], "fsdp", axis=0, tiled=True),
        lax.all_gather(params[1], "fsdp", axis=0, tiled=True),
        lax.all_gather(params[2], "fsdp", axis=0, tiled=True),
        lax.all_gather(params[3], "fsdp", axis=0, tiled=True),
        lax.all_gather(params[4], "fsdp", axis=0, tiled=True),
        lax.all_gather(params[5], "fsdp", axis=0, tiled=True),
    )


def reduce_grads(grads):
    pieces = (
        lax.psum_scatter(grads[0], "fsdp", scatter_dimension=0, tiled=True),
        lax.psum_scatter(grads[1], "fsdp", scatter_dimension=0, tiled=True),
        lax.psum_scatter(grads[2], "fsdp", scatter_dimension=0, tiled=True),
        lax.psum_scatter(grads[3], "fsdp", scatter_dimension=0, tiled=True),
        lax.psum_scatter(grads[4], "fsdp", scatter_dimension=0, tiled=True),
        lax.psum_scatter(grads[5], "fsdp", scatter_dimension=0, tiled=True),
    )
    return (
        lax.psum(pieces[0].astype(jnp.bfloat16), "dp").astype(jnp.float32),
        lax.psum(pieces[1].astype(jnp.bfloat16), "dp").astype(jnp.float32),
        lax.psum(pieces[2].astype(jnp.bfloat16), "dp").astype(jnp.float32),
        lax.psum(pieces[3].astype(jnp.bfloat16), "dp").astype(jnp.float32),
        lax.psum(pieces[4].astype(jnp.bfloat16), "dp").astype(jnp.float32),
        lax.psum(pieces[5].astype(jnp.bfloat16), "dp").astype(jnp.float32),
    )


def body(
    tokens,
    segment_ids,
    projection,
    norm1_gain,
    norm1_bias,
    qkv_weight,
    qkv_bias,
    out_weight,
    out_bias,
    norm2_gain,
    norm2_bias,
    in_weight,
    in_bias,
    ffn_out_weight,
    ffn_out_bias,
    cotangent,
):
    attn_local = (norm1_gain, norm1_bias, qkv_weight, qkv_bias, out_weight, out_bias)
    ffn_local = (norm2_gain, norm2_bias, in_weight, in_bias, ffn_out_weight, ffn_out_bias)
    model_width = tokens.shape[1]
    groups = lax.axis_size("fsdp")
    attn_full = fetch_block(attn_local)
    gain_one, shift_one, weight_qkv, bias_qkv, weight_out, bias_out = attn_full
    residual = tokens.astype(jnp.float32)
    normed_out_one, normed_one, inv_one = norm_forward(
        residual, gain_one.astype(jnp.float32), shift_one.astype(jnp.float32)
    )
    hidden_one = normed_out_one.astype(jnp.bfloat16)
    projected = jnp.dot(
        hidden_one, weight_qkv, preferred_element_type=jnp.float32
    ) + bias_qkv.astype(jnp.float32)
    attended = attend(projected, segment_ids, projection).astype(jnp.bfloat16)
    branch_one = jnp.dot(
        attended, weight_out, preferred_element_type=jnp.float32
    ) + bias_out.astype(jnp.float32)
    middle = residual + branch_one
    ffn_full = fetch_block(ffn_local)
    gain_two, shift_two, weight_in, bias_in, weight_ffo, bias_ffo = ffn_full
    normed_out_two, normed_two, inv_two = norm_forward(
        middle, gain_two.astype(jnp.float32), shift_two.astype(jnp.float32)
    )
    hidden_two = normed_out_two.astype(jnp.bfloat16)
    pre_act = jnp.dot(hidden_two, weight_in, preferred_element_type=jnp.float32) + bias_in.astype(
        jnp.float32
    )
    activated = jax.nn.gelu(pre_act, approximate=False).astype(jnp.bfloat16)
    branch_two = jnp.dot(
        activated, weight_ffo, preferred_element_type=jnp.float32
    ) + bias_ffo.astype(jnp.float32)
    output = (middle + branch_two).astype(jnp.bfloat16)
    upstream = cotangent.astype(jnp.float32)
    ffn_back = backward_weights(ffn_local)
    back_gain_two, unused_shift_two, back_in, unused_bias_in, back_ffo, unused_bias_ffo = ffn_back
    grad_ffo_weight = contract_rows(activated, cotangent)
    grad_ffo_bias = jnp.sum(upstream, axis=0)
    grad_activated = contract_cols(cotangent, back_ffo)
    slope = (
        0.5 * (1.0 + lax.erf(pre_act * 0.7071067811865476))
        + pre_act * jnp.exp(-0.5 * pre_act * pre_act) * 0.3989422804014327
    )
    grad_pre = (grad_activated * slope).astype(jnp.bfloat16)
    grad_in_weight = contract_rows(hidden_two, grad_pre)
    grad_in_bias = jnp.sum(grad_pre.astype(jnp.float32), axis=0)
    grad_hidden_two = contract_cols(grad_pre, back_in)
    back_two, grad_gain_two, grad_shift_two = norm_backward(
        grad_hidden_two, normed_two, inv_two, back_gain_two.astype(jnp.float32)
    )
    grad_middle = upstream + back_two
    ffn_grads = reduce_grads(
        (
            grad_gain_two,
            grad_shift_two,
            grad_in_weight,
            grad_in_bias,
            grad_ffo_weight,
            grad_ffo_bias,
        )
    )
    attn_back = backward_weights(attn_local)
    back_gain_one, unused_shift_one, back_qkv, unused_bias_qkv, back_out, unused_bias_out = (
        attn_back
    )
    grad_branch = grad_middle.astype(jnp.bfloat16)
    grad_out_weight = contract_rows(attended, grad_branch)
    grad_out_bias = jnp.sum(grad_branch.astype(jnp.float32), axis=0)
    grad_attended = contract_cols(grad_branch, back_out)
    grad_projected = attend_back(projected, segment_ids, projection, grad_attended).astype(
        jnp.bfloat16
    )
    grad_qkv_weight = contract_rows(hidden_one, grad_projected)
    grad_qkv_bias = jnp.sum(grad_projected.astype(jnp.float32), axis=0)
    bias_packed = jnp.concatenate(
        [
            grad_qkv_bias[: 2 * model_width].reshape(groups, -1),
            grad_qkv_bias[2 * model_width :].reshape(groups, -1),
        ],
        axis=1,
    ).reshape(-1)
    grad_hidden_one = contract_cols(grad_projected, back_qkv)
    back_one, grad_gain_one, grad_shift_one = norm_backward(
        grad_hidden_one, normed_one, inv_one, back_gain_one.astype(jnp.float32)
    )
    tokens_grad = (grad_middle + back_one).astype(jnp.bfloat16)
    attn_grads = reduce_grads(
        (
            grad_gain_one,
            grad_shift_one,
            grad_qkv_weight,
            bias_packed,
            grad_out_weight,
            grad_out_bias,
        )
    )
    owned_bias = attn_grads[3]
    split_point = 2 * model_width // groups
    return (
        output,
        tokens_grad,
        attn_grads[0],
        attn_grads[1],
        attn_grads[2],
        owned_bias[:split_point],
        owned_bias[split_point:],
        attn_grads[4],
        attn_grads[5],
        ffn_grads[0],
        ffn_grads[1],
        ffn_grads[2],
        ffn_grads[3],
        ffn_grads[4],
        ffn_grads[5],
    )


def solution(mesh):
    in_specs = (
        P(("fsdp", "dp"), None),
        P(("fsdp", "dp"), None),
        P(),
        P("fsdp"),
        P("fsdp"),
        P("fsdp", None),
        P("fsdp"),
        P("fsdp", None),
        P("fsdp"),
        P("fsdp"),
        P("fsdp"),
        P("fsdp", None),
        P("fsdp"),
        P("fsdp", None),
        P("fsdp"),
        P(("fsdp", "dp"), None),
    )
    out_specs = (
        P(("fsdp", "dp"), None),
        P(("fsdp", "dp"), None),
        P("fsdp"),
        P("fsdp"),
        P("fsdp", None),
        P("fsdp"),
        P("fsdp"),
        P("fsdp", None),
        P("fsdp"),
        P("fsdp"),
        P("fsdp"),
        P("fsdp", None),
        P("fsdp"),
        P("fsdp", None),
        P("fsdp"),
    )
    return jax.shard_map(body, mesh=mesh, in_specs=in_specs, out_specs=out_specs, check_vma=False)
```

profile of v0, /device:TPU:0, one launch (start us, length us, event | category | flops | bytes accessed | tf_op | source)
XLA Modules:
  0.0 792.6 jit_solution(11601006534894251956)
XLA Ops:
  22.0 63.5 %all-reduce.21 = (bf16[2304]{0:T(1024)(128)(2,1)S(1)}, bf16[768]{0:T(1024)(128)(2,1)S(1)}, bf16[768]{0:T(1024)(128)(2,1)S(1)}, bf16[768]{0:T(1024)(128)(2,1)}, b...) all-reduce(bf16[2304]{0:T(1024)(128)(2,1)S(1)} %dynamic-update-slic, ...), channel_id=1, replica_groups=mesh['fsdp'=16,'dp'=2] {'fsdp'}, use_global_device_ids=true, to_apply=%add.6 | all-reduce | flops 9984 | bytes 39936
  94.6 8.6 %convolution_add_fusion = f32[1024,2304]{1,0:T(8,128)} fusion(bf16[768,2304]{1,0:T(8,128)(2,1)} %all-gather.5.cloned.1.call-done, f32[2304]{0:T(1024)} %convert_element_type.162, bf16[1024,768]{0,1:T(8,128)(2,1)S(1)} %copy.55, f32[768]{0:T(1024)} %convert_element_type.160, f32[768]{0:T(1024)S(1)} %convert_element_type.159, f32[1024]{0:T(1024)S(1)} %add_rsqrt_fusion.1, ...), kind=kOutput, calls=%fused_computation.58 | convolution fusion | flops 3630956544 | bytes 14572544 | tf_op jit(solution)/shard_map/dot_general | solution.py:182
  103.3 9.7 %copy.56 = f32[1024,2304]{0,1:T(8,128)} copy(f32[1024,2304]{1,0:T(8,128)} %convolution_add_fusion) | data formatting | bytes 18874368 | tf_op jit(solution)/shard_map/add | solution.py:182
  122.1 21.6 %fusion.10 = f32[12,64,16,32]{1,3,2,0:T(8,128)S(1)} fusion(f32[1024,12,32]{0,2,1:T(8,128)S(1)} %get-tuple-element.162, f32[1024,16]{0,1:T(8,128)S(1)} %fusion.102, f32[1024,3,12,64]{0,3,2,1:T(8,128)S(1)} %bitcast.184), kind=kOutput, calls=%fused_computation.11 | convolution fusion | flops 4838129664 | bytes 6356992 | tf_op jit(solution)/shard_map/while/body/eval_jaxpr/nshf,nhd->shfd/dot_general | solution.py:57
  149.3 16.0 %fusion.4 = f32[12,1,1024,1]{2,1,3,0:T(1,128)S(1)} fusion(f32[16,12,32,1]{2,3,0,1:T(1,128)S(1)} %bitcast.190, f32[1024,12,32]{0,2,1:T(8,128)S(1)} %get-tuple-element.160, f32[1024,16]{0,1:T(8,128)S(1)} %fusion.102), kind=kOutput, calls=%fused_computation.4 | convolution fusion | flops 81788928 | bytes 1712128 | tf_op jit(solution)/shard_map/while/body/eval_jaxpr/nshf,shf->nh/dot_general | solution.py:62
  166.0 18.3 %fusion.65 = (bf16[1024,12,64]{0,2,1:T(8,128)(2,1)}, f32[12,64,1024,1]{2,1,3,0:T(8,128)}) fusion(f32[1024,12]{0,1:T(8,128)S(1)} %fusion.101, f32[1024,12,32]{0,2,1:T(8,128)S(1)} %get-tuple-element.160, f32[1024,16]{0,1:T(8,128)S(1)} %fusion.102, f32[12,64,16,32]{1,3,2,0:T(8,128)S(1)} %fusion.10), kind=kOutput, calls=%fused_computation.98 | convolution fusion | flops 4839702528 | bytes 7979008 | tf_op jit(solution)/shard_map/while/body/eval_jaxpr/nshf,shfd->nhd/dot_general | solution.py:60
  189.9 38.9 %fusion.16 = (bf16[1024,3072]{1,0:T(8,128)(2,1)}, f32[1024,3072]{1,0:T(8,128)}) fusion(f32[3072]{0:T(1024)S(1)} %copy-done.34, bf16[768,3072]{1,0:T(8,128)(2,1)} %all-gather.9.cloned.1.call-done, f32[1024,768]{0,1:T(8,128)} %copy-done.3, f32[768]{0:T(1024)S(1)} %copy-done.37, f32[768]{0:T(1024)S(1)} %convert_element_type.167, f32[1024]{0:T(1024)S(1)} %add_rsqrt_fusion, ...), kind=kOutput, calls=%fused_computation.21 | convolution fusion | flops 5043388416 | bytes 26765312 | tf_op jit(solution)/shard_map/dot_general | solution.py:196
  228.8 11.9 %convert_reduce_fusion = (f32[3072]{0:T(1024)S(1)}, bf16[1024,3072]{1,0:T(8,128)(2,1)S(1)}) fusion(f32[1024,3072]{1,0:T(8,128)} %get-tuple-element.169, f32[3072]{0:T(1024)S(1)} %copy-done.34, bf16[1024,768]{1,0:T(8,128)(2,1)S(1)} %copy-done.12, bf16[3072,768]{1,0:T(8,128)(2,1)} %all-gather.11.cloned.1.call-done), kind=kOutput, calls=%fused_computation.28 | convolution fusion | flops 4872729600 | bytes 25190400 | tf_op jit(solution)/shard_map/dot_general | solution.py:107
  240.8 6.8 fusion.123
  264.5 21.4 %fusion.2 = f32[12,64,16,32]{1,3,2,0:T(8,128)S(1)} fusion(f32[1024,12,32]{0,2,1:T(8,128)S(1)} %copy-done.18, f32[1024,16]{0,1:T(8,128)S(1)} %fusion.102, f32[1024,12,64]{0,2,1:T(8,128)S(1)} %bitcast.187, f32[1024,12]{0,1:T(8,128)S(1)} %copy-done.28), kind=kOutput, calls=%fused_computation.2 | convolution fusion | flops 4838916096 | bytes 6406144 | tf_op jit(solution)/shard_map/while/body/eval_jaxpr/transpose(jvp(nshf,shfd->nhd))/dot_general | solution.py:60
  286.8 49.4 %fusion = f32[12,1,16,32]{3,1,2,0:T(1,128)S(1)} fusion(f32[1024,12,32]{0,2,1:T(8,128)S(1)} %copy-done.18, f32[1024,16]{0,1:T(8,128)S(1)} %fusion.102, f32[12,1024,1,1]{1,0,2,3:T(8,128)S(1)} %get-tuple-element.155), kind=kOutput, calls=%fused_computation | convolution fusion | flops 81788928 | bytes 1712128 | tf_op jit(solution)/shard_map/while/body/eval_jaxpr/transpose(jvp(nshf,shf->nh))/dot_general | solution.py:62
  336.2 22.6 %multiply_reduce_fusion.1 = f32[12,1024,32]{1,2,0:T(8,128)S(1)} fusion(f32[12,16,32]{2,1,0:T(8,128)S(1)} %bitcast.191, f32[12,1024]{1,0:T(8,128)S(1)} %get-tuple-element.154, f32[1024,16]{0,1:T(8,128)S(1)} %fusion.102, f32[12,64,16,32]{1,3,2,0:T(8,128)S(1)} %copy-done.49, f32[1024,12,64]{0,2,1:T(8,128)S(1)} %bitcast.189, f32[1024,12]{0,1:T(8,128)S(1)} %copy-done.28), kind=kOutput, calls=%fused_computation.16 | convolution fusion | flops 4857397248 | bytes 6479872 | tf_op jit(solution)/shard_map/while/body/eval_jaxpr/transpose(jvp(nshf,shfd->nhd))/dot_general | solution.py:60
  358.8 22.8 %fusion.13 = f32[1024,12,32]{0,2,1:T(8,128)S(1)} fusion(f32[16,12,32]{2,0,1:T(8,128)S(1)} %bitcast.196, f32[1024,16]{0,1:T(8,128)S(1)} %fusion.102, f32[12,64,16,32]{1,3,2,0:T(8,128)S(1)} %fusion.2, f32[1024,3,12,64]{0,3,2,1:T(8,128)} %bitcast.181), kind=kOutput, calls=%fused_computation.15 | convolution fusion | flops 4850319360 | bytes 6381568 | tf_op jit(solution)/shard_map/while/body/eval_jaxpr/transpose(jvp(nshf,nhd->shfd))/dot_general | solution.py:57
  392.8 17.0 %fusion.71 = bf16[1024,1,12,64]{0,3,2,1:T(8,128)(2,1)S(1)} fusion(f32[12,64,16,32]{1,3,2,0:T(8,128)S(1)} %fusion.2, f32[1024,12,32]{0,2,1:T(8,128)S(1)} %copy-done.8, f32[1024,16]{0,1:T(8,128)S(1)} %fusion.102), kind=kOutput, calls=%fused_computation.115 | convolution fusion | flops 4838129664 | bytes 4784128 | tf_op jit(solution)/shard_map/while/body/eval_jaxpr/transpose(jvp(nshf,nhd->shfd))/dot_general | solution.py:57
  412.9 6.3 fusion.115
  419.3 10.7 %fusion.118 = f32[768,3072]{1,0:T(8,128)} fusion(bf16[1024,3072]{1,0:T(8,128)(2,1)} %copy-done.47, f32[1024,768]{0,1:T(8,128)} %copy-done.3, f32[768]{0:T(1024)S(1)} %copy-done.37, f32[768]{0:T(1024)S(1)} %convert_element_type.167, f32[1024]{0:T(1024)S(1)} %add_rsqrt_fusion, f32[1024]{0:T(1024)S(1)} %broadcast_multiply_fusion.4), kind=kOutput, calls=%fused_computation.196 | convolution fusion | flops 4835770368 | bytes 18888704 | tf_op jit(solution)/shard_map/dot_general | solution.py:101
  431.5 10.9 %fusion.124 = f32[3072,768]{1,0:T(8,128)} fusion(bf16[1024,3072]{1,0:T(8,128)(2,1)} %get-tuple-element.168, bf16[1024,768]{1,0:T(8,128)(2,1)S(1)} %copy-done.13), kind=kOutput, calls=%fused_computation.202 | convolution fusion | flops 4831838208 | bytes 17301504 | tf_op jit(solution)/shard_map/dot_general | solution.py:101
  444.8 9.8 %fusion.122 = (f32[768]{0:T(1024)S(1)}, f32[1024,768]{1,0:T(8,128)}) fusion(bf16[1024,2304]{0,1:T(8,128)(2,1)} %bitcast.186, bf16[768,2304]{1,0:T(8,128)(2,1)} %all-gather.5.cloned.1.call-done), kind=kOutput, calls=%fused_computation.200 | convolution fusion | flops 3624664320 | bytes 11406336 | tf_op jit(solution)/shard_map/dot_general | solution.py:107
  461.0 59.4 %all-reduce.20 = (bf16[2304]{0:T(1024)(128)(2,1)S(1)}, bf16[768]{0:T(1024)(128)(2,1)S(1)}, bf16[768]{0:T(1024)(128)(2,1)S(1)}, bf16[768]{0:T(1024)(128)(2,1)S(1)...) all-reduce(f32[2304]{0:T(1024)S(1)} %reshape.194, ...), channel_id=5, replica_groups=mesh['fsdp'=16,'dp'=2] {'fsdp'}, use_global_device_ids=true, to_apply=%region_23.25.clone | all-reduce | flops 9984 | bytes 59904
  521.0 4.9 all-reduce.22
  530.6 10.9 %add_convert_fusion = bf16[1024,768]{0,1:T(8,128)(2,1)} fusion(f32[1024,768]{0,1:T(8,128)} %copy-done.3, bf16[1024,3072]{1,0:T(8,128)(2,1)} %get-tuple-element.168, bf16[3072,768]{1,0:T(8,128)(2,1)} %all-gather.11.cloned.1.call-done, f32[768]{0:T(1024)S(1)} %convert_element_type.172), kind=kOutput, calls=%fused_computation.109 | convolution fusion | flops 4834197504 | bytes 15731712 | tf_op jit(solution)/shard_map/dot_general | solution.py:200
  544.9 77.4 %reduce-scatter.9.cloned.1.call-done = f32[48,3072]{1,0:T(8,128)} async-done(((f32[768,3072]{1,0:T(8,128)}), f32[48,3072]{1,0:T(8,128)}) %reduce-scatter.9.cloned.1.call-update) | async-done | bytes 589840 | tf_op jit(solution)/shard_map/reduce_scatter | solution.py:138
  624.2 114.0 %reduce-scatter.11.cloned.1.call-done = f32[192,768]{1,0:T(8,128)} async-done(((f32[3072,768]{1,0:T(8,128)}), f32[192,768]{1,0:T(8,128)}) %reduce-scatter.11.cloned.1.call-update) | async-done | bytes 589840 | tf_op jit(solution)/shard_map/reduce_scatter | solution.py:140
  747.0 31.6 %all-reduce.26.cloned.1.call-done = (bf16[48,2304]{1,0:T(8,128)(2,1)}, bf16[48,768]{1,0:T(8,128)(2,1)}, bf16[48,3072]{1,0:T(8,128)(2,1)}, bf16[192,768]{1,0:T(8,128)(2,1)}) async-done(((bf16[48,2304]{1,0:T(8,128)(2,1)}, bf16[48,768]{1,0:T(8,128)(2,1)}, bf16[48,3072]{1,0:T(8,128)(2,1)}, bf16[192,768]{1,0:T(8,128)(2,1)}), (bf16[48,2304]{1,0:T(8,128)(2,1)}, bf16[48,768]{1,0:T(8,128)(2,1)}, ...) | async-done | bytes 884752 | tf_op jit(solution)/shard_map/psum | solution.py:146
  (230 shorter events, 109.1 us)
Async XLA Ops:
  7.2 111.2 %copy-start = (f32[12,32,64]{2,1,0:T(8,128)S(1)}, f32[12,32,64]{2,1,0:T(8,128)}, u32[]{:S(2)}) copy-start(f32[12,32,64]{2,1,0:T(8,128)} %param.19) | copy-start | bytes 294916
  7.2 87.5 %all-gather.5.cloned.1.call-start = ((), (), s32[]{:S(2)}) async-start(), calls=%async_computation.4 | async-start | bytes 3760128 | tf_op jit(solution)/shard_map/all_gather | solution.py:116
  7.9 176.4 %all-gather.7.cloned.1.call-start = ((), (), s32[]{:S(2)}) async-start(), calls=%async_computation.5 | async-start | bytes 1253376 | tf_op jit(solution)/shard_map/all_gather | solution.py:118
  8.7 181.2 %all-gather.9.cloned.1.call-start = ((), (), s32[]{:S(2)}) async-start(), calls=%async_computation.6 | async-start | bytes 5013504 | tf_op jit(solution)/shard_map/all_gather | solution.py:116
  9.4 219.4 %all-gather.11.cloned.1.call-start = ((), (), s32[]{:S(2)}) async-start(), calls=%async_computation.7 | async-start | bytes 5013504 | tf_op jit(solution)/shard_map/all_gather | solution.py:118
  10.0 531.5 %reduce-scatter.7.cloned.1.call-start = ((), (), s32[]{:S(2)}) async-start(), calls=%async_computation.9 | async-start | bytes 2506752 | tf_op jit(solution)/shard_map/reduce_scatter | solution.py:140
  88.5 95.8 %copy-start.1 = (bf16[1024,768]{0,1:T(8,128)(2,1)}, bf16[1024,768]{0,1:T(8,128)(2,1)S(1)}, u32[]{:S(2)}) copy-start(bf16[1024,768]{0,1:T(8,128)(2,1)S(1)} %copy.55) | copy-start | bytes 4718596
  88.9 14.4 %copy-start.25 = (f32[1024]{0:T(1024)}, f32[1024]{0:T(1024)S(1)}, u32[]{:S(2)}) copy-start(f32[1024]{0:T(1024)S(1)} %broadcast_multiply_fusion.5) | copy-start | bytes 12292
  89.3 13.9 %copy-start.31 = (f32[1024]{0:T(1024)}, f32[1024]{0:T(1024)S(1)}, u32[]{:S(2)}) copy-start(f32[1024]{0:T(1024)S(1)} %add_rsqrt_fusion.1) | copy-start | bytes 12292
  90.6 26.3 %copy-start.19 = (f32[1024,32]{0,1:T(8,128)}, f32[1024,32]{0,1:T(8,128)S(1)}, u32[]{:S(2)}) copy-start(f32[1024,32]{0,1:T(8,128)S(1)} %get-tuple-element.158) | copy-start | bytes 393220
  122.0 21.6 %copy-start.7 = (f32[1024,12,32]{0,2,1:T(8,128)}, f32[1024,12,32]{0,2,1:T(8,128)S(1)}, u32[]{:S(2)}) copy-start(f32[1024,12,32]{0,2,1:T(8,128)S(1)} %get-tuple-element.162) | copy-start | bytes 4718596
  143.7 21.7 %copy-start.48 = (f32[12,64,16,32]{1,3,2,0:T(8,128)}, f32[12,64,16,32]{1,3,2,0:T(8,128)S(1)}, u32[]{:S(2)}) copy-start(f32[12,64,16,32]{1,3,2,0:T(8,128)S(1)} %fusion.10) | copy-start | bytes 4718596
  149.3 16.1 %copy-start.17 = (f32[1024,12,32]{0,2,1:T(8,128)}, f32[1024,12,32]{0,2,1:T(8,128)S(1)}, u32[]{:S(2)}) copy-start(f32[1024,12,32]{0,2,1:T(8,128)S(1)} %get-tuple-element.160) | copy-start | bytes 4718596
  149.3 16.0 %copy-start.33 = (f32[1024]{0:T(1024)S(1)}, f32[1024]{0:T(1024)}, u32[]{:S(2)}) copy-start(f32[1024]{0:T(1024)} %broadcast_subtract_fusion) | copy-start | bytes 12292
  166.0 18.3 %copy-start.38 = (f32[768]{0:T(1024)S(1)}, f32[768]{0:T(1024)}, u32[]{:S(2)}) copy-start(f32[768]{0:T(1024)} %convert_element_type.166) | copy-start | bytes 9220
  228.8 11.9 %copy-start.44 = (bf16[768,3072]{1,0:T(8,128)(2,1)S(1)}, bf16[768,3072]{1,0:T(8,128)(2,1)}, u32[]{:S(2)}) copy-start(bf16[768,3072]{1,0:T(8,128)(2,1)} %all-gather.9.cloned.1.call-done) | copy-start | bytes 14155780
  261.0 282.1 %reduce-scatter.5.cloned.1.call-start = ((), (), s32[]{:S(2)}) async-start(), calls=%async_computation.8 | async-start | bytes 7520256 | tf_op jit(solution)/shard_map/reduce_scatter | solution.py:138
  264.4 21.4 %copy-start.11 = (f32[12,64,1024,1]{2,1,3,0:T(8,128)S(1)}, f32[12,64,1024,1]{2,1,3,0:T(8,128)}, u32[]{:S(2)}) copy-start(f32[12,64,1024,1]{2,1,3,0:T(8,128)} %get-tuple-element.165) | copy-start | bytes 9437188
  286.8 49.4 %copy-start.24 = (f32[16,12,32]{2,0,1:T(8,128)S(1)}, f32[16,12,32]{2,0,1:T(8,128)}, u32[]{:S(2)}) copy-start(f32[16,12,32]{2,0,1:T(8,128)} %copy-done.23) | copy-start | bytes 73732
  286.8 49.4 %copy-start.49 = (f32[12,64,16,32]{1,3,2,0:T(8,128)S(1)}, f32[12,64,16,32]{1,3,2,0:T(8,128)}, u32[]{:S(2)}) copy-start(f32[12,64,16,32]{1,3,2,0:T(8,128)} %copy-done.48) | copy-start | bytes 4718596
  358.8 22.8 %copy-start.15 = (f32[12,1024,32]{1,2,0:T(8,128)S(1)}, f32[12,1024,32]{1,2,0:T(8,128)}, u32[]{:S(2)}) copy-start(f32[12,1024,32]{1,2,0:T(8,128)} %get-tuple-element.163) | copy-start | bytes 4718596
  419.2 203.1 %reduce-scatter.9.cloned.1.call-start = ((), (), s32[]{:S(2)}) async-start(), calls=%async_computation.10 | async-start | bytes 10027008 | tf_op jit(solution)/shard_map/reduce_scatter | solution.py:138
  430.0 308.2 %reduce-scatter.11.cloned.1.call-start = ((), (), s32[]{:S(2)}) async-start(), calls=%async_computation.11 | async-start | bytes 10027008 | tf_op jit(solution)/shard_map/reduce_scatter | solution.py:140
  442.4 336.2 %all-reduce.26.cloned.1.call-start = ((), (), s32[]{:S(2)}) async-start(), calls=%async_computation.12 | async-start | bytes 1769472 | tf_op jit(solution)/shard_map/psum | solution.py:146
  (38 other events, 134.4 us)
Sparse Core Ops, SparseCore 0:
  10.3 50.8 all-gather.4
  63.5 36.6 all-gather.6
  102.5 52.2 all-gather.8
  156.9 51.7 all-gather.10
  261.1 60.1 reduce-scatter.6
  419.3 87.8 reduce-scatter.4
  511.3 110.9 reduce-scatter.8
  627.0 111.0 reduce-scatter.10
  741.8 36.7 all-reduce.25
where the time goes:
time: 801 us; the launch traced here: 793 us
  matrix products  329 us (41%)
  waiting for transfers between devices  226 us (28%)
  blocking collectives  128 us (16%)
  local copies, waits for them, and re-layouts  46.5 us (6%)
  other arithmetic  44.3 us (6%)
  between operations  19.1 us (2%)
    unnamed x2, blocking collectives  123 us
    reduce_scatter x2, waiting for transfers between devices, reduce_grads(): lax.psum_scatter(grads[4], 'fsdp', scatter_dimension=0, tiled=True)  114 us
    reduce_scatter x2, waiting for transfers between devices, reduce_grads(): lax.psum_scatter(grads[2], 'fsdp', scatter_dimension=0, tiled=True)  77.4 us
    dot_general x2, matrix products, segment_core(): jnp.einsum('nshf,shf->nh', masked_queries, totals, precision=highest)  65.4 us
    dot_general x3, matrix products, segment_core(): jnp.einsum('nshf,shfd->nhd', masked_queries, kv_state, precision=highest)  62.4 us
    dot_general x3, matrix products, segment_core(): jnp.einsum('nshf,nhd->shfd', masked_keys, value_rows, precision=highest)  61.4 us
    dot_general x1, matrix products, body(): jnp.dot(hidden_two, weight_in, preferred_element_type=jnp.float32)  38.9 us
    dot_general x4, matrix products, contract_cols(): lax.dot_general(left, right, (((1,), (1,)), ((), ())), preferred_element_...  31.8 us
  transfers between devices with their start and end apart: 9, of which 3 were waited for; matrix products, arithmetic and copies ran while one was open for 47% of the time, Pallas kernels for 0%

commit v1 on v0

--- a/solution.py
+++ b/solution.py
@@ -143,7 +143,7 @@
     return (
         lax.psum(pieces[0].astype(jnp.bfloat16), "dp").astype(jnp.float32),
         lax.psum(pieces[1].astype(jnp.bfloat16), "dp").astype(jnp.float32),
-        lax.psum(pieces[2].astype(jnp.bfloat16), "dp").astype(jnp.float32),
+        jnp.sum(lax.all_gather(pieces[2].astype(jnp.bfloat16), "dp"), axis=0).astype(jnp.float32),
         lax.psum(pieces[3].astype(jnp.bfloat16), "dp").astype(jnp.float32),
         lax.psum(pieces[4].astype(jnp.bfloat16), "dp").astype(jnp.float32),
         lax.psum(pieces[5].astype(jnp.bfloat16), "dp").astype(jnp.float32),

time: 801 us -> 695 us (0.87)
  waiting for transfers between devices: 226 us -> 107 us
  blocking collectives: 128 us -> 145 us
    reduce_scatter x2, waiting for transfers between devices: 114 us -> 0.02 us  [reduce_grads(): lax.psum_scatter(grads[4], 'fsdp', scatter_dimension=0, tiled=True)]
    all_gather x0 -> x2, blocking collectives: none -> 16.9 us  [reduce_grads(): lax.all_gather(pieces[2].astype(jnp.bfloat16), 'dp')]
    psum x1, waiting for transfers between devices: 31.6 us -> 16.2 us  [reduce_grads(): lax.psum(pieces[4].astype(jnp.bfloat16), 'dp').astype(jnp.float32)]
    reduce_scatter x2, waiting for transfers between devices: 77.4 us -> 88.5 us  [reduce_grads(): lax.psum_scatter(grads[2], 'fsdp', scatter_dimension=0, tiled=True)]
    unnamed x135 -> x143, local copies, waits for them, and re-layouts: 24.5 us -> 25.4 us
  transfers between devices with their start and end apart: 9 -> 9, of which waited for: 3 -> 2; matrix products, arithmetic and copies ran while one was open for 47% -> 54% of each run, Pallas kernels for 0% -> 0%
where the time goes in v1:
time: 695 us; the launch traced here: 686 us
  matrix products  325 us (47%)
  blocking collectives  145 us (21%)
  waiting for transfers between devices  107 us (15%)
  local copies, waits for them, and re-layouts  47.7 us (7%)
  other arithmetic  40.4 us (6%)
  between operations  19.1 us (3%)
    unnamed x2, blocking collectives  124 us
    reduce_scatter x2, waiting for transfers between devices, reduce_grads(): lax.psum_scatter(grads[2], 'fsdp', scatter_dimension=0, tiled=True)  88.5 us
    dot_general x2, matrix products, segment_core(): jnp.einsum('nshf,shf->nh', masked_queries, totals, precision=highest)  65.2 us
    dot_general x3, matrix products, segment_core(): jnp.einsum('nshf,shfd->nhd', masked_queries, kv_state, precision=highest)  62.2 us
    dot_general x3, matrix products, segment_core(): jnp.einsum('nshf,nhd->shfd', masked_keys, value_rows, precision=highest)  60.8 us
    dot_general x1, matrix products, body(): jnp.dot(hidden_two, weight_in, preferred_element_type=jnp.float32)  38.9 us
    dot_general x4, matrix products, contract_cols(): lax.dot_general(left, right, (((1,), (1,)), ((), ())), preferred_element_...  32 us
    dot_general x4, matrix products, contract_rows(): lax.dot_general(left, right, (((0,), (0,)), ((), ())), preferred_element_...  30.3 us
  transfers between devices with their start and end apart: 9, of which 2 were waited for; matrix products, arithmetic and copies ran while one was open for 54% of the time, Pallas kernels for 0%

profile of v1, /device:TPU:0, one launch (start us, length us, event | category | flops | bytes accessed | tf_op | source)
XLA Modules:
  0.0 685.7 jit_solution(5106083203645284273)
XLA Ops:
  22.0 63.5 %all-reduce.21 = (bf16[2304]{0:T(1024)(128)(2,1)S(1)}, bf16[768]{0:T(1024)(128)(2,1)S(1)}, bf16[768]{0:T(1024)(128)(2,1)S(1)}, bf16[768]{0:T(1024)(128)(2,1)}, b...) all-reduce(bf16[2304]{0:T(1024)(128)(2,1)S(1)} %dynamic-update-slic, ...), channel_id=1, replica_groups=mesh['fsdp'=16,'dp'=2] {'fsdp'}, use_global_device_ids=true, to_apply=%add.6 | all-reduce | flops 9984 | bytes 39936
  94.6 8.6 %convolution_add_fusion = f32[1024,2304]{1,0:T(8,128)} fusion(bf16[768,2304]{1,0:T(8,128)(2,1)} %all-gather.7.cloned.1.call-done, f32[2304]{0:T(1024)} %convert_element_type.166, bf16[1024,768]{0,1:T(8,128)(2,1)S(1)} %copy.55, f32[768]{0:T(1024)} %convert_element_type.164, f32[768]{0:T(1024)S(1)} %convert_element_type.163, f32[1024]{0:T(1024)S(1)} %add_rsqrt_fusion.1, ...), kind=kOutput, calls=%fused_computation.58 | convolution fusion | flops 3630956544 | bytes 14572544 | tf_op jit(solution)/shard_map/dot_general | solution.py:182
  103.2 9.6 %copy.56 = f32[1024,2304]{0,1:T(8,128)} copy(f32[1024,2304]{1,0:T(8,128)} %convolution_add_fusion) | data formatting | bytes 18874368 | tf_op jit(solution)/shard_map/add | solution.py:182
  121.9 21.4 %fusion.10 = f32[12,64,16,32]{1,3,2,0:T(8,128)S(1)} fusion(f32[1024,12,32]{0,2,1:T(8,128)S(1)} %get-tuple-element.160, f32[1024,16]{0,1:T(8,128)S(1)} %fusion.102, f32[1024,3,12,64]{0,3,2,1:T(8,128)S(1)} %bitcast.186), kind=kOutput, calls=%fused_computation.11 | convolution fusion | flops 4838129664 | bytes 6356992 | tf_op jit(solution)/shard_map/while/body/eval_jaxpr/nshf,nhd->shfd/dot_general | solution.py:57
  148.9 16.0 %fusion.4 = f32[12,1,1024,1]{2,1,3,0:T(1,128)S(1)} fusion(f32[16,12,32,1]{2,3,0,1:T(1,128)S(1)} %bitcast.194, f32[1024,12,32]{0,2,1:T(8,128)S(1)} %get-tuple-element.158, f32[1024,16]{0,1:T(8,128)S(1)} %fusion.102), kind=kOutput, calls=%fused_computation.4 | convolution fusion | flops 81788928 | bytes 1712128 | tf_op jit(solution)/shard_map/while/body/eval_jaxpr/nshf,shf->nh/dot_general | solution.py:62
  165.0 18.6 %fusion.65 = (bf16[1024,12,64]{0,2,1:T(8,128)(2,1)}, f32[12,64,1024,1]{2,1,3,0:T(8,128)}) fusion(f32[1024,12]{0,1:T(8,128)S(1)} %fusion.101, f32[1024,12,32]{0,2,1:T(8,128)S(1)} %get-tuple-element.158, f32[1024,16]{0,1:T(8,128)S(1)} %fusion.102, f32[12,64,16,32]{1,3,2,0:T(8,128)S(1)} %fusion.10), kind=kOutput, calls=%fused_computation.98 | convolution fusion | flops 4839702528 | bytes 7979008 | tf_op jit(solution)/shard_map/while/body/eval_jaxpr/nshf,shfd->nhd/dot_general | solution.py:60
  189.2 38.9 %fusion.16 = (bf16[1024,3072]{1,0:T(8,128)(2,1)}, f32[1024,3072]{1,0:T(8,128)}) fusion(f32[3072]{0:T(1024)S(1)} %copy-done.36, bf16[768,3072]{1,0:T(8,128)(2,1)} %all-gather.11.cloned.1.call-done, f32[1024,768]{0,1:T(8,128)} %copy-done.3, f32[768]{0:T(1024)S(1)} %copy-done.41, f32[768]{0:T(1024)S(1)} %convert_element_type.171, f32[1024]{0:T(1024)S(1)} %add_rsqrt_fusion, ...), kind=kOutput, calls=%fused_computation.21 | convolution fusion | flops 5043388416 | bytes 26765312 | tf_op jit(solution)/shard_map/dot_general | solution.py:196
  228.1 12.5 %convert_reduce_fusion = (f32[3072]{0:T(1024)}, bf16[1024,3072]{1,0:T(8,128)(2,1)S(1)}) fusion(f32[1024,3072]{1,0:T(8,128)} %get-tuple-element.167, f32[3072]{0:T(1024)S(1)} %copy-done.36, bf16[1024,768]{1,0:T(8,128)(2,1)S(1)} %copy-done.15, bf16[3072,768]{1,0:T(8,128)(2,1)} %all-gather.13.cloned.1.call-done), kind=kOutput, calls=%fused_computation.28 | convolution fusion | flops 4872729600 | bytes 25190400 | tf_op jit(solution)/shard_map/dot_general | solution.py:107
  240.6 7.3 %fusion.123 = (f32[768]{0:T(1024)}, f32[1024,768]{1,0:T(8,128)}) fusion(bf16[1024,3072]{1,0:T(8,128)(2,1)S(1)} %get-tuple-element.173, bf16[768,3072]{1,0:T(8,128)(2,1)S(1)} %copy-done.49), kind=kOutput, calls=%fused_computation.201 | convolution fusion | flops 4832623616 | bytes 14158848 | tf_op jit(solution)/shard_map/dot_general | solution.py:107
  261.3 10.3 %fusion.124 = f32[3072,768]{1,0:T(8,128)} fusion(bf16[1024,3072]{1,0:T(8,128)(2,1)} %get-tuple-element.166, bf16[1024,768]{1,0:T(8,128)(2,1)S(1)} %copy-done.16), kind=kOutput, calls=%fused_computation.202 | convolution fusion | flops 4831838208 | bytes 17301504 | tf_op jit(solution)/shard_map/dot_general | solution.py:101
  277.9 49.1 %fusion = f32[12,1,16,32]{3,1,2,0:T(1,128)S(1)} fusion(f32[1024,12,32]{0,2,1:T(8,128)S(1)} %copy-done.20, f32[1024,16]{0,1:T(8,128)S(1)} %fusion.102, f32[12,1024,1,1]{1,0,2,3:T(8,128)S(1)} %get-tuple-element.153), kind=kOutput, calls=%fused_computation | convolution fusion | flops 81788928 | bytes 1712128 | tf_op jit(solution)/shard_map/while/body/eval_jaxpr/transpose(jvp(nshf,shf->nh))/dot_general | solution.py:62
  327.0 20.8 %fusion.2 = f32[12,64,16,32]{1,3,2,0:T(8,128)S(1)} fusion(f32[1024,12,32]{0,2,1:T(8,128)S(1)} %copy-done.20, f32[1024,16]{0,1:T(8,128)S(1)} %fusion.102, f32[1024,12,64]{0,2,1:T(8,128)S(1)} %bitcast.190, f32[1024,12]{0,1:T(8,128)S(1)} %copy-done.30), kind=kOutput, calls=%fused_computation.2 | convolution fusion | flops 4838916096 | bytes 6406144 | tf_op jit(solution)/shard_map/while/body/eval_jaxpr/transpose(jvp(nshf,shfd->nhd))/dot_general | solution.py:60
  347.8 22.9 %fusion.13 = f32[1024,12,32]{0,2,1:T(8,128)S(1)} fusion(f32[16,12,32]{2,0,1:T(8,128)S(1)} %bitcast.200, f32[1024,16]{0,1:T(8,128)S(1)} %fusion.102, f32[12,64,16,32]{1,3,2,0:T(8,128)S(1)} %fusion.2, f32[1024,3,12,64]{0,3,2,1:T(8,128)} %bitcast.183), kind=kOutput, calls=%fused_computation.15 | convolution fusion | flops 4850319360 | bytes 6381568 | tf_op jit(solution)/shard_map/while/body/eval_jaxpr/transpose(jvp(nshf,nhd->shfd))/dot_general | solution.py:57
  374.7 22.9 %multiply_reduce_fusion.1 = f32[12,1024,32]{1,2,0:T(8,128)S(1)} fusion(f32[12,16,32]{2,1,0:T(8,128)S(1)} %bitcast.195, f32[12,1024]{1,0:T(8,128)S(1)} %get-tuple-element.152, f32[1024,16]{0,1:T(8,128)S(1)} %fusion.102, f32[12,64,16,32]{1,3,2,0:T(8,128)S(1)} %copy-done.53, f32[1024,12,64]{0,2,1:T(8,128)S(1)} %bitcast.191, f32[1024,12]{0,1:T(8,128)S(1)} %copy-done.30), kind=kOutput, calls=%fused_computation.16 | convolution fusion | flops 4857397248 | bytes 6479872 | tf_op jit(solution)/shard_map/while/body/eval_jaxpr/transpose(jvp(nshf,shfd->nhd))/dot_general | solution.py:60
  404.1 16.5 %fusion.71 = bf16[1024,1,12,64]{0,3,2,1:T(8,128)(2,1)S(1)} fusion(f32[12,64,16,32]{1,3,2,0:T(8,128)S(1)} %fusion.2, f32[1024,12,32]{0,2,1:T(8,128)S(1)} %copy-done.11, f32[1024,16]{0,1:T(8,128)S(1)} %fusion.102), kind=kOutput, calls=%fused_computation.115 | convolution fusion | flops 4838129664 | bytes 4784128 | tf_op jit(solution)/shard_map/while/body/eval_jaxpr/transpose(jvp(nshf,nhd->shfd))/dot_general | solution.py:57
  423.8 6.4 fusion.115
  430.8 10.8 %fusion.118 = f32[768,3072]{1,0:T(8,128)} fusion(bf16[1024,3072]{1,0:T(8,128)(2,1)} %copy-done.51, f32[1024,768]{0,1:T(8,128)} %copy-done.3, f32[768]{0:T(1024)S(1)} %copy-done.42, f32[768]{0:T(1024)S(1)} %convert_element_type.171, f32[1024]{0:T(1024)S(1)} %add_rsqrt_fusion, f32[1024]{0:T(1024)S(1)} %broadcast_multiply_fusion.4), kind=kOutput, calls=%fused_computation.196 | convolution fusion | flops 4835770368 | bytes 18888704 | tf_op jit(solution)/shard_map/dot_general | solution.py:101
  444.1 9.4 %fusion.122 = (f32[768]{0:T(1024)S(1)}, f32[1024,768]{1,0:T(8,128)}) fusion(bf16[1024,2304]{0,1:T(8,128)(2,1)} %bitcast.188, bf16[768,2304]{1,0:T(8,128)(2,1)} %all-gather.7.cloned.1.call-done), kind=kOutput, calls=%fused_computation.200 | convolution fusion | flops 3624664320 | bytes 11406336 | tf_op jit(solution)/shard_map/dot_general | solution.py:107
  463.8 8.6 %add_convert_fusion = bf16[1024,768]{0,1:T(8,128)(2,1)S(1)} fusion(f32[1024,768]{0,1:T(8,128)S(1)} %copy-done.5, bf16[1024,3072]{1,0:T(8,128)(2,1)} %get-tuple-element.166, bf16[3072,768]{1,0:T(8,128)(2,1)} %all-gather.13.cloned.1.call-done, f32[768]{0:T(1024)S(1)} %convert_element_type.176), kind=kOutput, calls=%fused_computation.109 | convolution fusion | flops 4834197504 | bytes 15731712 | tf_op jit(solution)/shard_map/dot_general | solution.py:200
  476.1 60.0 %all-reduce.20 = (bf16[2304]{0:T(1024)(128)(2,1)S(1)}, bf16[768]{0:T(1024)(128)(2,1)S(1)}, bf16[768]{0:T(1024)(128)(2,1)S(1)}, bf16[768]{0:T(1024)(128)(2,1)S(1)...) all-reduce(f32[2304]{0:T(1024)S(1)} %reshape.194, ...), channel_id=7, replica_groups=mesh['fsdp'=16,'dp'=2] {'fsdp'}, use_global_device_ids=true, to_apply=%region_23.25.clone | all-reduce | flops 9984 | bytes 59904
  550.6 6.6 all-gather
  558.2 88.5 %reduce-scatter.9.cloned.1.call-done = f32[48,3072]{1,0:T(8,128)} async-done(((f32[768,3072]{1,0:T(8,128)}), f32[48,3072]{1,0:T(8,128)}) %reduce-scatter.9.cloned.1.call-update) | async-done | bytes 589840 | tf_op jit(solution)/shard_map/reduce_scatter | solution.py:138
  647.7 10.3 %all-gather.1 = bf16[96,3072]{1,0:T(8,128)(2,1)S(1)} all-gather(bf16[48,3072]{1,0:T(8,128)(2,1)S(1)} %convert_element_type.202), channel_id=3, replica_groups=mesh['fsdp'=16,'dp'=2] {'dp'}, dimensions={0}, use_global_device_ids=true | all-gather | bytes 884736 | tf_op jit(solution)/shard_map/all_gather | solution.py:146
  659.1 16.2 %all-reduce.26.cloned.1.call-done = (bf16[48,768]{1,0:T(8,128)(2,1)}, bf16[192,768]{1,0:T(8,128)(2,1)}) async-done(((bf16[48,768]{1,0:T(8,128)(2,1)}, bf16[192,768]{1,0:T(8,128)(2,1)}), (bf16[48,768]{1,0:T(8,128)(2,1)}, bf16[192,768]{1,0:T(8,128)(2,1)})) %all-reduce.26.cloned.1.call-update) | async-done | bytes 368656 | tf_op jit(solution)/shard_map/psum | solution.py:148
  (242 shorter events, 111.0 us)
Async XLA Ops:
  7.2 111.0 %copy-start = (f32[12,32,64]{2,1,0:T(8,128)S(1)}, f32[12,32,64]{2,1,0:T(8,128)}, u32[]{:S(2)}) copy-start(f32[12,32,64]{2,1,0:T(8,128)} %param.19) | copy-start | bytes 294916
  7.2 87.4 %all-gather.7.cloned.1.call-start = ((), (), s32[]{:S(2)}) async-start(), calls=%async_computation.4 | async-start | bytes 3760128 | tf_op jit(solution)/shard_map/all_gather | solution.py:116
  7.9 175.7 %all-gather.9.cloned.1.call-start = ((), (), s32[]{:S(2)}) async-start(), calls=%async_computation.5 | async-start | bytes 1253376 | tf_op jit(solution)/shard_map/all_gather | solution.py:118
  8.7 180.5 %all-gather.11.cloned.1.call-start = ((), (), s32[]{:S(2)}) async-start(), calls=%async_computation.6 | async-start | bytes 5013504 | tf_op jit(solution)/shard_map/all_gather | solution.py:116
  9.4 218.7 %all-gather.13.cloned.1.call-start = ((), (), s32[]{:S(2)}) async-start(), calls=%async_computation.7 | async-start | bytes 5013504 | tf_op jit(solution)/shard_map/all_gather | solution.py:118
  10.0 462.5 %reduce-scatter.7.cloned.1.call-start = ((), (), s32[]{:S(2)}) async-start(), calls=%async_computation.9 | async-start | bytes 2506752 | tf_op jit(solution)/shard_map/reduce_scatter | solution.py:140
  88.5 95.1 %copy-start.1 = (bf16[1024,768]{0,1:T(8,128)(2,1)}, bf16[1024,768]{0,1:T(8,128)(2,1)S(1)}, u32[]{:S(2)}) copy-start(bf16[1024,768]{0,1:T(8,128)(2,1)S(1)} %copy.55) | copy-start | bytes 4718596
  88.9 14.3 %copy-start.27 = (f32[1024]{0:T(1024)}, f32[1024]{0:T(1024)S(1)}, u32[]{:S(2)}) copy-start(f32[1024]{0:T(1024)S(1)} %broadcast_multiply_fusion.5) | copy-start | bytes 12292
  89.3 13.8 %copy-start.33 = (f32[1024]{0:T(1024)}, f32[1024]{0:T(1024)S(1)}, u32[]{:S(2)}) copy-start(f32[1024]{0:T(1024)S(1)} %add_rsqrt_fusion.1) | copy-start | bytes 12292
  90.6 26.1 %copy-start.21 = (f32[1024,32]{0,1:T(8,128)}, f32[1024,32]{0,1:T(8,128)S(1)}, u32[]{:S(2)}) copy-start(f32[1024,32]{0,1:T(8,128)S(1)} %get-tuple-element.156) | copy-start | bytes 393220
  121.9 21.4 %copy-start.10 = (f32[1024,12,32]{0,2,1:T(8,128)}, f32[1024,12,32]{0,2,1:T(8,128)S(1)}, u32[]{:S(2)}) copy-start(f32[1024,12,32]{0,2,1:T(8,128)S(1)} %get-tuple-element.160) | copy-start | bytes 4718596
  143.3 21.7 %copy-start.52 = (f32[12,64,16,32]{1,3,2,0:T(8,128)}, f32[12,64,16,32]{1,3,2,0:T(8,128)S(1)}, u32[]{:S(2)}) copy-start(f32[12,64,16,32]{1,3,2,0:T(8,128)S(1)} %fusion.10) | copy-start | bytes 4718596
  148.9 16.1 %copy-start.19 = (f32[1024,12,32]{0,2,1:T(8,128)}, f32[1024,12,32]{0,2,1:T(8,128)S(1)}, u32[]{:S(2)}) copy-start(f32[1024,12,32]{0,2,1:T(8,128)S(1)} %get-tuple-element.158) | copy-start | bytes 4718596
  148.9 16.0 %copy-start.35 = (f32[1024]{0:T(1024)S(1)}, f32[1024]{0:T(1024)}, u32[]{:S(2)}) copy-start(f32[1024]{0:T(1024)} %broadcast_subtract_fusion) | copy-start | bytes 12292
  165.0 18.6 %copy-start.29 = (f32[1024,12]{0,1:T(8,128)}, f32[1024,12]{0,1:T(8,128)S(1)}, u32[]{:S(2)}) copy-start(f32[1024,12]{0,1:T(8,128)S(1)} %fusion.101) | copy-start | bytes 147460
  165.0 18.6 %copy-start.43 = (f32[768]{0:T(1024)S(1)}, f32[768]{0:T(1024)}, u32[]{:S(2)}) copy-start(f32[768]{0:T(1024)} %convert_element_type.170) | copy-start | bytes 9220
  228.1 12.5 %copy-start.49 = (bf16[768,3072]{1,0:T(8,128)(2,1)S(1)}, bf16[768,3072]{1,0:T(8,128)(2,1)}, u32[]{:S(2)}) copy-start(bf16[768,3072]{1,0:T(8,128)(2,1)} %all-gather.11.cloned.1.call-done) | copy-start | bytes 14155780
  261.2 212.9 %reduce-scatter.11.cloned.1.call-start = ((), (), s32[]{:S(2)}) async-start(), calls=%async_computation.11 | async-start | bytes 10027008 | tf_op jit(solution)/shard_map/reduce_scatter | solution.py:140
  271.6 277.9 %reduce-scatter.5.cloned.1.call-start = ((), (), s32[]{:S(2)}) async-start(), calls=%async_computation.8 | async-start | bytes 7520256 | tf_op jit(solution)/shard_map/reduce_scatter | solution.py:138
  277.9 49.1 %copy-start.30 = (f32[1024,12]{0,1:T(8,128)S(1)}, f32[1024,12]{0,1:T(8,128)}, u32[]{:S(2)}) copy-start(f32[1024,12]{0,1:T(8,128)} %copy-done.29) | copy-start | bytes 147460
  347.8 22.9 %copy-start.18 = (f32[12,1024,32]{1,2,0:T(8,128)S(1)}, f32[12,1024,32]{1,2,0:T(8,128)}, u32[]{:S(2)}) copy-start(f32[12,1024,32]{1,2,0:T(8,128)} %get-tuple-element.161) | copy-start | bytes 4718596
  374.7 22.9 %copy-start.17 = (f32[12,1024,32]{1,2,0:T(8,128)S(1)}, f32[12,1024,32]{1,2,0:T(8,128)}, u32[]{:S(2)}) copy-start(f32[12,1024,32]{1,2,0:T(8,128)} %get-tuple-element.159) | copy-start | bytes 4718596
  430.2 216.5 %reduce-scatter.9.cloned.1.call-start = ((), (), s32[]{:S(2)}) async-start(), calls=%async_computation.10 | async-start | bytes 10027008 | tf_op jit(solution)/shard_map/reduce_scatter | solution.py:138
  441.6 233.7 %all-reduce.26.cloned.1.call-start = ((), (), s32[]{:S(2)}) async-start(), calls=%async_computation.12 | async-start | bytes 737280 | tf_op jit(solution)/shard_map/psum | solution.py:148
  (42 other events, 166.6 us)
Sparse Core Ops, SparseCore 0:
  10.3 50.8 all-gather.6
  63.5 36.6 all-gather.8
  102.5 52.3 all-gather.10
  157.0 51.7 all-gather.12
  261.3 60.1 reduce-scatter.6
  326.1 110.3 reduce-scatter.10
  440.5 90.3 reduce-scatter.4
  535.6 111.0 reduce-scatter.8
  650.1 25.1 all-reduce.25
